TPU v7x, 128 devices: a whole 4x4x4 slice. The times are simulated.
128 devices in a mesh: tm: 32 (over z, y, core), chan: 4 (over x).
Axes of the slice: x: 4, y: 4, z: 4, core: 2. Of those that a mesh axis runs over, the one named last changes fastest.
Arguments:
- coarse: bfloat16 [2, 98304, 4096], P(None, 'tm', 'chan'), may hold values from -6 to 6
- prototype: float32 [16, 1024], replicated, may hold values from -4 to 4
- req_block: int32 [4, 4], replicated, may hold values from 0 to 31, as said below
- req_start: int32 [4, 4], replicated, may hold values from 0 to 80, as said below
- req_frames: int32 [4, 4], replicated, may hold values from 1 to 81
- req_count: int32 [4], replicated, may hold values from 1 to 4, as said below
Outputs:
- spectra: bfloat16 [96, 4, 4, 2, 1024, 128], P('tm', 'chan')
Inputs may be any that keep to these rules, and one draw needn't show every extreme that they name: `req_block`: among the live slots of one owner at most 2 name blocks b with the same b // 8; in every draw some owner reaches 2. req_start + req_frames <= 81 in every slot; in every draw some live slot starts at hop 81 - 1 and some live slot spans all 81 frames. Slots q < req_count[c] of owner c are live, the others are empty; in every draw some owner has 4 live slots.
All inputs are finite; a program needn't handle non-finite values.
Results may differ from a plain program's by a relative error of at most 0.001.
Values may be sent and summed in bfloat16 or wider, within the bound.
No kernel may reach another device: no remote copies, remote signals or barrier semaphores. Data moves between devices by JAX's collectives and lax.ppermute only.
A program may use at most 256 MiB of HBM per device.

v0:
```python
import math

import jax
import jax.numpy as jnp
import ml_dtypes
import numpy as np
from jax import lax
from jax.experimental import pallas as pl
from jax.experimental.pallas import tpu as pltpu
from jax.sharding import PartitionSpec as P

BLOCKW = 128
NFINE = 1024
TAPS = 16
HOPS_DEV = 3
MAXREQ = 4
PAIR = 2
TM = 32
OWNERS = 4
BPC = 8
HOPS = 96
HALF = BLOCKW // 2
SHARE = HALF // TM
ROWS = 8
RADIX = 8
LANES = 128
FRAMES = 84
GROUP = 42
COST = pl.CostEstimate(flops=18_000_000_000, transcendentals=0, bytes_accessed=2 * MAXREQ * HOPS * 4 * NFINE * 2)


def share_pick():
    shape = (TM * ROWS, 2 * BLOCKW)
    row, column = (lax.broadcasted_iota(jnp.int32, shape, dim) for dim in range(2))
    place = (row // ROWS) * SHARE + row % SHARE + HALF * ((row // 4) % 2) + BLOCKW * ((row // 2) % 2)
    return jnp.where(place == column, 1.0, 0.0).astype(jnp.bfloat16)


def late_pick():
    shape = (TM * ROWS, PAIR * 2 * BLOCKW)
    row, column = (lax.broadcasted_iota(jnp.int32, shape, dim) for dim in range(2))
    place = HALF + (row // ROWS) * SHARE + row % SHARE + BLOCKW * ((row // 4) % 2) + 2 * BLOCKW * ((row // 2) % 2)
    return jnp.where(place == column, 1.0, 0.0).astype(jnp.bfloat16)


def dft_tables():
    k2 = np.arange(LANES)[None, :, None]
    m = np.arange(RADIX)[:, None, None] + RADIX * np.arange(LANES)[None, None, :]
    angles = (k2 * m % NFINE) * (2.0 * math.pi / NFINE)
    table = np.concatenate([np.cos(angles), np.sin(angles)], axis=2) / math.sqrt(NFINE)
    high = table.astype(np.float32).astype(ml_dtypes.bfloat16)
    low = (table - high.astype(np.float64)).astype(np.float32).astype(ml_dtypes.bfloat16)
    return high, low


def wanted_block(shift, rank, block_ref, count_ref, place_ref):
    owner = (place_ref[0] + shift) % OWNERS
    seen = jnp.int32(0)
    chosen = jnp.int32(0)
    for slot in range(MAXREQ):
        block = block_ref[owner, slot]
        mine = (slot < count_ref[owner]) & (block // BPC == place_ref[0])
        chosen = jnp.where(mine & (seen == rank), block % BPC, chosen)
        seen = seen + mine.astype(jnp.int32)
    return seen > rank, chosen


def some_serves_all(block_ref, count_ref):
    some = jnp.bool_(False)
    for source in range(OWNERS):
        every = jnp.bool_(True)
        for owner in range(OWNERS):
            serves = jnp.bool_(False)
            for slot in range(MAXREQ):
                serves = serves | ((slot < count_ref[owner]) & (block_ref[owner, slot] // BPC == source))
            every = every & serves
        some = some | every
    return some


def pack_kernel(block_ref, count_ref, place_ref, x_ref, *refs):
    plan_ref, late_ref, last_ref, *early_refs = refs[: 3 + OWNERS]
    block_buf, late_buf, early_buf, pick_ref, block_sem, late_sem, early_sem = refs[3 + OWNERS :]
    wanted = [[wanted_block(d, r, block_ref, count_ref, place_ref) for r in range(PAIR)] for d in range(OWNERS)]
    groups = []
    live = jnp.int32(0)
    for d in range(OWNERS):
        groups.append(live)
        plan_ref[d] = live
        live = live + wanted[d][0][0].astype(jnp.int32)

    def block_copy(d, r):
        columns = pl.ds(pl.multiple_of(wanted[d][r][1] * BLOCKW, BLOCKW), BLOCKW)
        return pltpu.make_async_copy(x_ref.at[:, :, columns], block_buf.at[d, r], block_sem.at[d, r])

    def start_late_copy(d):
        @pl.when(groups[d] < OWNERS - 1)
        def _():
            pltpu.make_async_copy(late_buf.at[d], late_ref.at[:, groups[d]], late_sem.at[d]).start()

        @pl.when(groups[d] == OWNERS - 1)
        def _():
            pltpu.make_async_copy(late_buf.at[d], last_ref.at[:, 0], late_sem.at[d]).start()

    def early_copy(d, r):
        return pltpu.make_async_copy(early_buf.at[d, r], early_refs[d].at[r], early_sem.at[d, r])

    order = [(d, r) for d in (1, 2, 3, 0) for r in range(PAIR)]
    for d, r in order:
        pl.when(wanted[d][r][0])(lambda d=d, r=r: block_copy(d, r).start())
    pick_ref[...] = late_pick()
    plan_ref[OWNERS] = some_serves_all(block_ref, count_ref).astype(jnp.int32)
    for d, r in order:
        if r == 0:
            pl.when(wanted[d][0][0])(lambda d=d: block_copy(d, 0).wait())
            continue

        pl.when(wanted[d][1][0])(lambda d=d: block_copy(d, 1).wait())
        for rank in range(PAIR):

            @pl.when(wanted[d][rank][0])
            def _():
                early_buf[d, rank] = jnp.concatenate(
                    [block_buf[d, rank, 0, :, :HALF], block_buf[d, rank, 1, :, :HALF]], axis=1
                ).reshape(HOPS_DEV, NFINE, BLOCKW)
                early_copy(d, rank).start()

        def turn_blocks(d, ranks):
            def one_hop(hop, carry):
                rows = pl.ds(pl.multiple_of(hop * NFINE, NFINE), NFINE)
                wide = jnp.concatenate([block_buf[d, i // 2, i % 2, rows] for i in range(2 * ranks)], axis=1)
                turned = lax.dot_general(
                    pick_ref[:, : 2 * ranks * BLOCKW],
                    wide,
                    (((1,), (1,)), ((), ())),
                    preferred_element_type=jnp.float32,
                )
                late_buf[d, :, hop] = turned.reshape(TM, ROWS, NFINE).astype(jnp.bfloat16)
                return carry

            lax.fori_loop(0, HOPS_DEV, one_hop, 0)
            start_late_copy(d)

        pl.when(wanted[d][1][0])(lambda d=d: turn_blocks(d, 2))
        pl.when(wanted[d][0][0] & jnp.logical_not(wanted[d][1][0]))(lambda d=d: turn_blocks(d, 1))

    for d, r in order:
        pl.when(wanted[d][r][0])(lambda d=d, r=r: early_copy(d, r).wait())
        if r == 0:
            pl.when(wanted[d][0][0])(
                lambda d=d: pltpu.make_async_copy(late_buf.at[d], last_ref.at[:, 0], late_sem.at[d]).wait()
            )


def pack(coarse, req_block, req_count, place):
    anywhere = pl.BlockSpec(memory_space=pl.ANY)
    early = jax.ShapeDtypeStruct((PAIR, HOPS_DEV, NFINE, BLOCKW), jnp.bfloat16)
    return pl.pallas_call(
        pack_kernel,
        out_shape=[
            jax.ShapeDtypeStruct((OWNERS + 1,), jnp.int32),
            jax.ShapeDtypeStruct((TM, OWNERS - 1, HOPS_DEV, ROWS, NFINE), jnp.bfloat16),
            jax.ShapeDtypeStruct((TM, 1, HOPS_DEV, ROWS, NFINE), jnp.bfloat16),
        ]
        + [early] * OWNERS,
        grid_spec=pltpu.PrefetchScalarGridSpec(
            num_scalar_prefetch=3,
            grid=(1,),
            in_specs=[anywhere],
            out_specs=[pl.BlockSpec(memory_space=pltpu.SMEM)] + [anywhere] * (2 + OWNERS),
            scratch_shapes=[
                pltpu.VMEM((OWNERS, PAIR, 2, HOPS_DEV * NFINE, BLOCKW), jnp.bfloat16),
                pltpu.VMEM((OWNERS, TM, HOPS_DEV, ROWS, NFINE), jnp.bfloat16),
                pltpu.VMEM((OWNERS, PAIR, HOPS_DEV, NFINE, BLOCKW), jnp.bfloat16),
                pltpu.VMEM((TM * ROWS, PAIR * 2 * BLOCKW), jnp.bfloat16),
                pltpu.SemaphoreType.DMA((OWNERS, PAIR)),
                pltpu.SemaphoreType.DMA((OWNERS,)),
                pltpu.SemaphoreType.DMA((OWNERS, PAIR)),
            ],
        ),
        name="pack",
    )(req_block, req_count, place, coarse)


def in_vmem(array):
    return pltpu.with_memory_space_constraint(array, pltpu.VMEM)


def in_hbm(array):
    return pltpu.with_memory_space_constraint(array, pltpu.HBM)


def split_kernel(plan_ref, late_ref, last_ref, *refs):
    out_refs, sem = refs[:-1], refs[-1]
    for d, out_ref in enumerate(out_refs, 1):
        group = plan_ref[d]

        @pl.when(group < OWNERS - 1)
        def _():
            pltpu.make_async_copy(late_ref.at[:, group], out_ref, sem.at[d]).start()

        @pl.when(group >= OWNERS - 1)
        def _():
            pltpu.make_async_copy(last_ref.at[:, 0], out_ref, sem.at[d]).start()

    for d, out_ref in enumerate(out_refs, 1):
        pltpu.make_async_copy(last_ref.at[:, 0], out_ref, sem.at[d]).wait()


def split(plan, late, last):
    anywhere = pl.BlockSpec(memory_space=pl.ANY)
    return pl.pallas_call(
        split_kernel,
        out_shape=[jax.ShapeDtypeStruct((TM, HOPS_DEV, ROWS, NFINE), jnp.bfloat16)] * (OWNERS - 1),
        grid_spec=pltpu.PrefetchScalarGridSpec(
            num_scalar_prefetch=1,
            grid=(1,),
            in_specs=[anywhere] * 2,
            out_specs=[anywhere] * (OWNERS - 1),
            scratch_shapes=[pltpu.SemaphoreType.DMA((OWNERS,))],
        ),
        name="split",
    )(plan, in_hbm(late), in_hbm(last))


def arrival(slot, block_ref, count_ref, place_ref):
    owner = place_ref[0]
    slot = jnp.where(slot < count_ref[owner], slot, 0)
    source = block_ref[owner, slot] // BPC
    rank = jnp.int32(0)
    for other in range(MAXREQ - 1):
        same = (other < slot) & (block_ref[owner, other] // BPC == source)
        rank = rank + same.astype(jnp.int32)
    return (owner - source + OWNERS) % OWNERS, jnp.minimum(rank, PAIR - 1)


def choose_kernel(block_ref, count_ref, place_ref, a0, a1, a2, a3, out_ref, held_ref, out_buf, pick_ref, held_sem, out_sem):
    for slot in range(MAXREQ):
        shift, rank = arrival(slot, block_ref, count_ref, place_ref)
        for own, ref in enumerate((a0, a1, a2, a3)):

            @pl.when(shift == own)
            def _():
                pltpu.make_async_copy(ref.at[rank], held_ref.at[slot], held_sem.at[slot]).start()

    pick_ref[...] = share_pick()

    def out_copy(pair, hop):
        return pltpu.make_async_copy(out_buf.at[pair, hop], out_ref.at[:, pair, hop], out_sem.at[pair, hop])

    for pair in range(MAXREQ // 2):
        for slot in (2 * pair, 2 * pair + 1):
            pltpu.make_async_copy(a0.at[0], held_ref.at[slot], held_sem.at[slot]).wait()
        for hop in range(HOPS_DEV):
            both = jnp.concatenate([held_ref[pair * 2, hop], held_ref[pair * 2 + 1, hop]], axis=1)
            turned = lax.dot_general(
                pick_ref[...], both, (((1,), (1,)), ((), ())), preferred_element_type=jnp.float32
            )
            out_buf[pair, hop] = turned.reshape(TM, ROWS, NFINE).astype(jnp.bfloat16)
            out_copy(pair, hop).start()
    for pair in range(MAXREQ // 2):
        for hop in range(HOPS_DEV):
            out_copy(pair, hop).wait()


def choose(arrived, req_block, req_count, place):
    anywhere = pl.BlockSpec(memory_space=pl.ANY)
    return pl.pallas_call(
        choose_kernel,
        out_shape=jax.ShapeDtypeStruct((TM, MAXREQ // 2, HOPS_DEV, ROWS, NFINE), jnp.bfloat16),
        grid_spec=pltpu.PrefetchScalarGridSpec(
            num_scalar_prefetch=3,
            grid=(1,),
            in_specs=[anywhere] * OWNERS,
            out_specs=anywhere,
            scratch_shapes=[
                pltpu.VMEM((MAXREQ, HOPS_DEV, NFINE, BLOCKW), jnp.bfloat16),
                pltpu.VMEM((MAXREQ // 2, HOPS_DEV, TM, ROWS, NFINE), jnp.bfloat16),
                pltpu.VMEM((TM * ROWS, 2 * BLOCKW), jnp.bfloat16),
                pltpu.SemaphoreType.DMA((MAXREQ,)),
                pltpu.SemaphoreType.DMA((MAXREQ // 2, HOPS_DEV)),
            ],
        ),
        cost_estimate=pl.CostEstimate(flops=150_000_000_000, transcendentals=0, bytes_accessed=2**22),
        name="choose",
    )(req_block, req_count, place, *map(in_hbm, arrived))


def turn(value, sign):
    return pltpu.roll(value, ROWS // 2, value.ndim - 2) * sign


def dft4(a, b, c, d, sign):
    s02, d02, s13, d13 = a + c, a - c, b + d, turn(b - d, sign)
    return s02 + s13, d02 + d13, s02 - s13, d02 - d13


def dft8(x, sign):
    half = math.sqrt(0.5)
    low = [x[i] + x[i + 4] for i in range(4)]
    high = [x[i] - x[i + 4] for i in range(4)]
    high[1] = (high[1] + turn(high[1], sign)) * half
    high[2] = turn(high[2], sign)
    high[3] = (turn(high[3], sign) - high[3]) * half
    even, odd = dft4(*low, sign), dft4(*high, sign)
    return [pair for both in zip(even, odd) for pair in both]


def transform(load, proto_ref, high_ref, low_ref, out_ref, wide_ref, fir_ref):
    sign = jnp.where(lax.broadcasted_iota(jnp.int32, (ROWS, LANES), 0) < ROWS // 2, 1.0, -1.0)
    wide_ref[:, HOPS:] = jnp.zeros((RADIX, FRAMES + TAPS - 1 - HOPS, ROWS, LANES), jnp.float32)

    def widen(tile, carry):
        wide_ref[tile, :HOPS] = load(pl.ds(pl.multiple_of(tile * LANES, LANES), LANES))
        return carry

    lax.fori_loop(0, RADIX, widen, 0)

    def one_group(group):
        first = group * GROUP
        for tile in range(RADIX):
            lanes = slice(tile * LANES, (tile + 1) * LANES)
            total = None
            for tap in range(TAPS):
                weights = jnp.broadcast_to(proto_ref[tap, lanes].reshape(1, LANES), (ROWS, LANES))
                part = wide_ref[tile, pl.ds(first + tap, GROUP)] * weights
                total = part if total is None else total + part
            fir_ref[group, tile] = total
        for frame in range(0, GROUP, 2):
            parts = [fir_ref[group, tile, frame : frame + 2] for tile in range(RADIX)]
            for m1, value in enumerate(dft8(parts, sign)):
                fir_ref[group, m1, frame : frame + 2] = value
        for m1 in range(RADIX):
            value = fir_ref[group, m1].reshape(GROUP * ROWS, LANES)
            top = value.astype(jnp.bfloat16)
            rest = (value - top.astype(jnp.float32)).astype(jnp.bfloat16)
            high = high_ref[m1]
            product = jnp.dot(
                jnp.concatenate([top, rest, top], axis=1),
                jnp.concatenate([high, high, low_ref[m1]], axis=0),
                preferred_element_type=jnp.float32,
            )
            cosines = product[:, :LANES].reshape(GROUP, ROWS, LANES)
            sines = product[:, LANES:].reshape(GROUP, ROWS, LANES)
            result = (cosines + turn(sines, sign)).astype(jnp.bfloat16)
            devices = GROUP // HOPS_DEV
            out_ref[pl.ds(group * devices, devices), :, 0, :, m1 * LANES : (m1 + 1) * LANES] = result.reshape(
                devices, HOPS_DEV, ROWS, LANES
            )

    for group in range(FRAMES // GROUP):
        one_group(group)


def early_kernel(x_ref, *refs):
    pair = pl.program_id(0)

    def load(lanes):
        return x_ref[:, pair, :, :, lanes].astype(jnp.float32).reshape(HOPS, ROWS, LANES)

    transform(load, *refs)


def late_kernel(block_ref, count_ref, place_ref, a0, a1, a2, a3, proto_ref, high_ref, low_ref, out_ref, wide_ref, fir_ref, held_ref, sem):
    pair = pl.program_id(0)

    @pl.when(pair == 0)
    def _():
        for slot in range(MAXREQ):
            shift, _ = arrival(slot, block_ref, count_ref, place_ref)
            for own, ref in enumerate((a0.at[:, 0], a1, a2, a3)):

                @pl.when(shift == own)
                def _():
                    pltpu.make_async_copy(ref, held_ref.at[slot], sem.at[slot]).start()

    for slot in range(2):
        at = pair * 2 + slot
        pltpu.make_async_copy(a1, held_ref.at[at], sem.at[at]).wait()

    ranks = [arrival(slot, block_ref, count_ref, place_ref)[1] for slot in range(MAXREQ)]
    first_rank = jnp.where(pair == 0, ranks[0], ranks[2])
    second_rank = jnp.where(pair == 0, ranks[1], ranks[3])
    is_second = (lax.broadcasted_iota(jnp.int32, (HOPS, ROWS, LANES), 1) // SHARE) % 2 == 1

    def load(lanes):
        first = held_ref[pair * 2, :, :, :, lanes].astype(jnp.float32).reshape(HOPS, ROWS, LANES)
        second = held_ref[pair * 2 + 1, :, :, :, lanes].astype(jnp.float32).reshape(HOPS, ROWS, LANES)
        first = jnp.where(first_rank == 0, first, pltpu.roll(first, ROWS - SHARE, 1))
        second = jnp.where(second_rank == 1, second, pltpu.roll(second, SHARE, 1))
        return jnp.where(is_second, second, first)

    transform(load, proto_ref, high_ref, low_ref, out_ref, wide_ref, fir_ref)


def table_specs():
    return [
        pl.BlockSpec((TAPS, NFINE), lambda p, *refs: (0, 0)),
        pl.BlockSpec((RADIX, LANES, 2 * LANES), lambda p, *refs: (0, 0, 0)),
        pl.BlockSpec((RADIX, LANES, 2 * LANES), lambda p, *refs: (0, 0, 0)),
    ]


RESULT = jax.ShapeDtypeStruct((TM, HOPS_DEV, MAXREQ // 2, ROWS, NFINE), jnp.bfloat16)


def result_spec():
    return pl.BlockSpec((TM, HOPS_DEV, 1, ROWS, NFINE), lambda p, *refs: (0, 0, p, 0, 0))


def work_space():
    return [
        pltpu.VMEM((RADIX, FRAMES + TAPS - 1, ROWS, LANES), jnp.float32),
        pltpu.VMEM((FRAMES // GROUP, RADIX, GROUP, ROWS, LANES), jnp.float32),
    ]


def filter_early(gathered, tables):
    return pl.pallas_call(
        early_kernel,
        out_shape=RESULT,
        grid=(MAXREQ // 2,),
        in_specs=[
            pl.BlockSpec(memory_space=pltpu.VMEM),
            *table_specs(),
        ],
        out_specs=result_spec(),
        scratch_shapes=work_space(),
        cost_estimate=COST,
        name="filter_early",
    )(in_vmem(gathered), *tables)


def filter_late(arrived, tables, req_block, req_count, place):
    return pl.pallas_call(
        late_kernel,
        out_shape=RESULT,
        grid_spec=pltpu.PrefetchScalarGridSpec(
            num_scalar_prefetch=3,
            grid=(MAXREQ // 2,),
            in_specs=[pl.BlockSpec(memory_space=pl.ANY)] * OWNERS + table_specs(),
            out_specs=result_spec(),
            scratch_shapes=work_space()
            + [
                pltpu.VMEM((MAXREQ, TM, HOPS_DEV, ROWS, NFINE), jnp.bfloat16),
                pltpu.SemaphoreType.DMA((MAXREQ,)),
            ],
        ),
        cost_estimate=COST,
        compiler_params=pltpu.CompilerParams(vmem_limit_bytes=56 * 2**20),
        name="filter_late",
    )(req_block, req_count, place, *map(in_hbm, arrived), *tables)


def is_active(hop, slot, start_ref, frames_ref, count_ref, place_ref):
    owner = place_ref[0]
    frame = place_ref[1] * HOPS_DEV + hop
    begin = start_ref[owner, slot]
    return (slot < count_ref[owner]) & (frame >= begin) & (frame < begin + frames_ref[owner, slot])


def turn_back(back, pick_ref, turned_ref):
    rows = back.astype(jnp.float32).reshape(TM * ROWS, NFINE).astype(jnp.bfloat16)
    columns = lax.dot_general(rows, pick_ref[...], (((0,), (0,)), ((), ())), preferred_element_type=jnp.float32)
    for m1 in range(RADIX):
        for slot in range(2):
            turned_ref[slot, pl.ds(m1, LANES, stride=RADIX), :] = columns[
                m1 * LANES : (m1 + 1) * LANES, slot * BLOCKW : (slot + 1) * BLOCKW
            ]


def unpack_early_kernel(start_ref, frames_ref, count_ref, place_ref, early_ref, out_ref, turned_ref, pick_ref):
    refs = start_ref, frames_ref, count_ref, place_ref
    step = pl.program_id(0)
    hop, pair = step // (MAXREQ // 2), step % (MAXREQ // 2)

    @pl.when(step == 0)
    def _():
        pick_ref[...] = share_pick()

    @pl.when(is_active(hop, 2 * pair, *refs) | is_active(hop, 2 * pair + 1, *refs))
    def _():
        turn_back(early_ref[:, 0, 0], pick_ref, turned_ref)
        out_ref[0] = turned_ref[...].astype(jnp.bfloat16)


def unpack_kernel(start_ref, frames_ref, count_ref, place_ref, part_ref, late_ref, out_ref, turned_ref, pick_ref):
    refs = start_ref, frames_ref, count_ref, place_ref
    step = pl.program_id(0)
    hop, pair = step // (MAXREQ // 2), step % (MAXREQ // 2)

    @pl.when(step == 0)
    def _():
        pick_ref[...] = share_pick()

    @pl.when(is_active(hop, 2 * pair, *refs) | is_active(hop, 2 * pair + 1, *refs))
    def _():
        turn_back(late_ref[:, hop, pair], pick_ref, turned_ref)

    for which in range(2):
        active = is_active(hop, 2 * pair + which, *refs)

        @pl.when(active)
        def _():
            early = part_ref[0, which]
            late = turned_ref[which].astype(jnp.bfloat16)
            out_ref[0, 0, which, 0] = jnp.concatenate([early[:, :HALF], late[:, :HALF]], axis=1)
            out_ref[0, 0, which, 1] = jnp.concatenate([early[:, HALF:], late[:, HALF:]], axis=1)

        @pl.when(jnp.logical_not(active))
        def _():
            out_ref[0, 0, which] = jnp.zeros((2, NFINE, BLOCKW), jnp.bfloat16)


STEPS = HOPS_DEV * MAXREQ // 2


def unpack_early(early, req_start, req_frames, req_count, place):
    return pl.pallas_call(
        unpack_early_kernel,
        out_shape=jax.ShapeDtypeStruct((STEPS, 2, NFINE, BLOCKW), jnp.bfloat16),
        grid_spec=pltpu.PrefetchScalarGridSpec(
            num_scalar_prefetch=4,
            grid=(STEPS,),
            in_specs=[pl.BlockSpec((TM, 1, 1, ROWS, NFINE), lambda i, *refs: (0, i // (MAXREQ // 2), i % (MAXREQ // 2), 0, 0))],
            out_specs=pl.BlockSpec((1, 2, NFINE, BLOCKW), lambda i, *refs: (i, 0, 0, 0)),
            scratch_shapes=[
                pltpu.VMEM((2, NFINE, BLOCKW), jnp.float32),
                pltpu.VMEM((TM * ROWS, 2 * BLOCKW), jnp.bfloat16),
            ],
        ),
        cost_estimate=COST,
        compiler_params=pltpu.CompilerParams(vmem_limit_bytes=52 * 2**20),
        name="unpack_early",
    )(req_start, req_frames, req_count, place, in_hbm(early))


def unpack(part, late, req_start, req_frames, req_count, place):
    resident = pl.BlockSpec(memory_space=pltpu.VMEM)
    return pl.pallas_call(
        unpack_kernel,
        out_shape=jax.ShapeDtypeStruct((HOPS_DEV, 1, MAXREQ, 2, NFINE, BLOCKW), jnp.bfloat16),
        grid_spec=pltpu.PrefetchScalarGridSpec(
            num_scalar_prefetch=4,
            grid=(STEPS,),
            in_specs=[pl.BlockSpec((1, 2, NFINE, BLOCKW), lambda i, *refs: (i, 0, 0, 0)), resident],
            out_specs=pl.BlockSpec(
                (1, 1, 2, 2, NFINE, BLOCKW),
                lambda i, *refs: (i // (MAXREQ // 2), 0, i % (MAXREQ // 2), 0, 0, 0),
            ),
            scratch_shapes=[
                pltpu.VMEM((2, NFINE, BLOCKW), jnp.float32),
                pltpu.VMEM((TM * ROWS, 2 * BLOCKW), jnp.bfloat16),
            ],
        ),
        compiler_params=pltpu.CompilerParams(vmem_limit_bytes=52 * 2**20),
        name="unpack",
    )(req_start, req_frames, req_count, place, in_hbm(part), in_vmem(late))


def over_tm(array):
    return lax.all_to_all(array, "tm", split_axis=0, concat_axis=0, tiled=True)


def along_chan(arrays):
    return [arrays[0]] + [
        lax.ppermute(in_hbm(arrays[d]), "chan", [(s, (s + d) % OWNERS) for s in range(OWNERS)])
        for d in range(1, OWNERS)
    ]


def shards(coarse, prototype, req_block, req_start, req_frames, req_count):
    column = lax.axis_index("chan").astype(jnp.int32)
    place = jnp.stack([column, lax.axis_index("tm").astype(jnp.int32)])
    tables = (prototype, *(jnp.asarray(table) for table in dft_tables()))
    plan, late, last, *early = pack(coarse, req_block, req_count, place)
    late = over_tm(late)
    late, last = lax.optimization_barrier((late, last))
    last = lax.cond(plan[OWNERS] > 0, over_tm, lambda same: same, last)
    early = choose(along_chan(early), req_block, req_count, place)
    late, last, early = lax.optimization_barrier((late, last, early))
    early = over_tm(early)
    late = along_chan([late, *split(plan, late, last)])
    early = filter_early(early, tables)
    _, *late = lax.optimization_barrier((early, *late))
    early = over_tm(early)
    _, late = lax.optimization_barrier((early, filter_late(late, tables, req_block, req_count, place)))
    late = over_tm(late)
    part = unpack_early(early, req_start, req_frames, req_count, place)
    return unpack(part, late, req_start, req_frames, req_count, place)


def solution(mesh):
    return jax.shard_map(
        shards,
        mesh=mesh,
        in_specs=(P(None, "tm", "chan"), P(), P(), P(), P(), P()),
        out_specs=P("tm", "chan", None, None, None, None),
        check_vma=False,
    )
```

profile of v0, /device:TPU:0, one launch (start us, length us, event | category | flops | bytes accessed | tf_op | source)
XLA Modules:
  0.0 389.3 jit_solution(3326712670445310008)
XLA Ops:
  0.0 0.6 pad_add_fusion.place_ref
  0.6 7.3 %pack.1 = (s32[5]{0:T(128)}, bf16[32,3,3,8,1024]{4,3,2,1,0:T(8,128)(2,1)}, bf16[32,1,3,8,1024]{4,3,2,1,0:T(8,128)(2,1)}, bf16[2,3,1024,128]{3,2,1,0:T(8,128)(2,1...) custom-call(s32[4,4]{1,0:T(4,128)} %block_ref.5, ...), custom_call_target="tpu_custom_call" | custom-call | tf_op jit(solution)/shard_map/pack/pallas_call | solution.py:158
  8.0 0.9 collective-permute-start
  8.9 6.0 %collective-permute-start.1 = (bf16[2,3,1024,128]{3,2,1,0:T(8,128)(2,1)}, bf16[2,3,1024,128]{3,2,1,0:T(8,128)(2,1)}, u32[]{:S(2)}, u32[]{:S(2)}) collective-permute-start(bf16[2,3,1024,128]{3,2,1,0:T(8,128)(2,1)} %get-tuple-element.37), channel_id=1, source_target_pairs={{0,2},{1,3},{2,0},{3,1},{4,6},{5,7},{6,4},{7,5},{8,10},{9,11},{10,... | collective-permute-start | bytes 4718600 | tf_op jit(solution)/shard_map/ppermute | solution.py:567
  14.8 8.6 %all-to-all-start.1 = ((bf16[32,3,3,8,1024]{4,3,2,1,0:T(8,128)(2,1)}), bf16[32,3,3,8,1024]{4,3,2,1,0:T(8,128)(2,1)}, u32[]{:S(2)}, u32[]{:S(2)}) async-start(bf16[32,3,3,8,1024]{4,3,2,1,0:T(8,128)(2,1)} %get-tuple-element.30), calls=%async_computation.1 | async-start | bytes 9437184 | tf_op jit(solution)/shard_map/all_to_all | solution.py:562
  23.4 0.7 slice.3
  24.8 23.2 %collective-permute-done.a1 = bf16[2,3,1024,128]{3,2,1,0:T(8,128)(2,1)S(1)} collective-permute-done((bf16[2,3,1024,128]{3,2,1,0:T(8,128)(2,1)}, bf16[2,3,1024,128]{3,2,1,0:T(8,128)(2,1)S(1)}, u32[]{:S(2)}, u32[]{:S(2)}) %collective-permute-start) | collective-permute-done | bytes 1572896 | tf_op jit(solution)/shard_map/ppermute | solution.py:567
  48.0 35.0 %collective-permute-done.1.a2 = bf16[2,3,1024,128]{3,2,1,0:T(8,128)(2,1)} collective-permute-done((bf16[2,3,1024,128]{3,2,1,0:T(8,128)(2,1)}, bf16[2,3,1024,128]{3,2,1,0:T(8,128)(2,1)}, u32[]{:S(2)}, u32[]{:S(2)}) %collective-permute-start.1) | collective-permute-done | bytes 1572896 | tf_op jit(solution)/shard_map/ppermute | solution.py:567
  83.0 0.0 collective-permute-done.2.a3
  83.0 4.4 %choose.1 = bf16[32,2,3,8,1024]{4,3,2,1,0:T(8,128)(2,1)} custom-call(s32[4,4]{1,0:T(4,128)} %block_ref.5, s32[4]{0:T(128)} %count_ref.9, s32[2]{0:T(128)} %pad_add_fusion.place_ref, bf16[2,3,1024,128]{3,2,1,0:T(8,128)(2,1)} %get-tuple-element.35.a0, bf16[2,3,1024,128]{3,2,1,0:T(8,128)(2,1)} %copy-done.8, ...), custom_call_target="tpu_custom_call" | custom-call | flops 149999992832 | bytes 4194304 | tf_op jit(solution)/shard_map/choose/pallas_call | solution.py:268
  87.4 0.0 all-to-all-done.1.late_ref.a0
  87.5 0.0 copy-start.5
  87.5 1.1 copy-done.5
  88.6 8.3 %all-to-all-start.2 = ((bf16[32,2,3,8,1024]{4,3,2,1,0:T(8,128)(2,1)}), bf16[32,2,3,8,1024]{4,3,2,1,0:T(8,128)(2,1)S(1)}, u32[]{:S(2)}, u32[]{:S(2)}) async-start(bf16[32,2,3,8,1024]{4,3,2,1,0:T(8,128)(2,1)} %choose.1), calls=%async_computation.2 | async-start | bytes 6291456 | tf_op jit(solution)/shard_map/all_to_all | solution.py:562
  97.0 144.7 %split.1 = (bf16[32,3,8,1024]{3,2,1,0:T(8,128)(2,1)}, bf16[32,3,8,1024]{3,2,1,0:T(8,128)(2,1)}, bf16[32,3,8,1024]{3,2,1,0:T(8,128)(2,1)}) custom-call(s32[5]{0:T(128)} %get-tuple-element.33.plan_ref, bf16[32,3,3,8,1024]{4,3,2,1,0:T(8,128)(2,1)} %all-to-all-done.1.late_ref.a0, bf16[32,1,3,8,1024]{4,3,2,1,0:T(8,128)(2,1)} %copy-done.5), custom_call_target="tpu_custom_call" | custom-call | tf_op jit(solution)/shard_map/split/pallas_call | solution.py:212
  241.7 0.1 collective-permute-start.3
  241.8 4.2 %collective-permute-start.4 = (bf16[32,3,8,1024]{3,2,1,0:T(8,128)(2,1)}, bf16[32,3,8,1024]{3,2,1,0:T(8,128)(2,1)}, u32[]{:S(2)}, u32[]{:S(2)}) collective-permute-start(bf16[32,3,8,1024]{3,2,1,0:T(8,128)(2,1)} %get-tuple-element.43), channel_id=1, source_target_pairs={{0,2},{1,3},{2,0},{3,1},{4,6},{5,7},{6,4},{7,5},{8,10},{9,11},{10,... | collective-permute-start | bytes 4718600 | tf_op jit(solution)/shard_map/ppermute | solution.py:567
  246.0 0.0 collective-permute-start.5
  246.0 12.4 %filter_early.1 = bf16[32,3,2,8,1024]{4,3,2,1,0:T(8,128)(2,1)} custom-call(bf16[32,2,3,8,1024]{4,3,2,1,0:T(8,128)(2,1)S(1)} %all-to-all-done.2.x_ref, f32[16,1024]{1,0:T(8,128)} %proto_ref.1, bf16[8,128,256]{2,1,0:T(8,128)(2,1)} %constant.16.clone.refs_1_.high_ref, bf16[8,128,256]{2,1,0:T(8,128)(2,1)} %constant.17.clone.refs_2_.low_ref), custom_call_target="tpu_custom_call" | custom-call | flops 17999998976 | bytes 6291456 | tf_op jit(solution)/shard_map/filter_early/pallas_call | solution.py:419
  258.4 7.4 %all-to-all-start.3 = ((bf16[32,3,2,8,1024]{4,3,2,1,0:T(8,128)(2,1)}), bf16[32,3,2,8,1024]{4,3,2,1,0:T(8,128)(2,1)S(1)}, u32[]{:S(2)}, u32[]{:S(2)}) async-start(bf16[32,3,2,8,1024]{4,3,2,1,0:T(8,128)(2,1)} %filter_early.1), calls=%async_computation.3 | async-start | bytes 6291456 | tf_op jit(solution)/shard_map/all_to_all | solution.py:562
  265.8 14.1 %collective-permute-done.3.a1 = bf16[32,3,8,1024]{3,2,1,0:T(8,128)(2,1)} collective-permute-done((bf16[32,3,8,1024]{3,2,1,0:T(8,128)(2,1)}, bf16[32,3,8,1024]{3,2,1,0:T(8,128)(2,1)}, u32[]{:S(2)}, u32[]{:S(2)}) %collective-permute-start.3) | collective-permute-done | bytes 1572896 | tf_op jit(solution)/shard_map/ppermute | solution.py:567
  279.9 34.7 %collective-permute-done.4.a2 = bf16[32,3,8,1024]{3,2,1,0:T(8,128)(2,1)} collective-permute-done((bf16[32,3,8,1024]{3,2,1,0:T(8,128)(2,1)}, bf16[32,3,8,1024]{3,2,1,0:T(8,128)(2,1)}, u32[]{:S(2)}, u32[]{:S(2)}) %collective-permute-start.4) | collective-permute-done | bytes 1572896 | tf_op jit(solution)/shard_map/ppermute | solution.py:567
  314.6 17.1 %filter_late.1 = bf16[32,3,2,8,1024]{4,3,2,1,0:T(8,128)(2,1)} custom-call(s32[4,4]{1,0:T(4,128)} %block_ref.5, s32[4]{0:T(128)} %count_ref.9, s32[2]{0:T(128)} %pad_add_fusion.place_ref, bf16[32,3,3,8,1024]{4,3,2,1,0:T(8,128)(2,1)} %all-to-all-done.1.late_ref.a0, bf16[32,3,8,1024]{3,2,1,0:T(8,128)(2,1)} %collective-permute-done.3.a1, ...), custom_call_target="tpu_custom_call" | custom-call | flops 17999998976 | bytes 6291456 | tf_op jit(solution)/shard_map/filter_late/pallas_call | solution.py:435
  331.7 0.0 copy-start
  331.7 0.0 copy-start.1
  331.7 0.0 copy-start.2
  331.8 0.0 copy-start.6
  331.8 1.7 copy-done.6
  333.4 7.2 %all-to-all-start.4 = ((bf16[32,3,2,8,1024]{4,3,2,1,0:T(8,128)(2,1)}), bf16[32,3,2,8,1024]{4,3,2,1,0:T(8,128)(2,1)S(1)}, u32[]{:S(2)}, u32[]{:S(2)}) async-start(bf16[32,3,2,8,1024]{4,3,2,1,0:T(8,128)(2,1)} %filter_late.1), calls=%async_computation.4 | async-start | bytes 6291456 | tf_op jit(solution)/shard_map/all_to_all | solution.py:562
  340.7 5.9 %unpack_early.1.part_ref = bf16[6,2,1024,128]{3,2,1,0:T(8,128)(2,1)} custom-call(s32[4,4]{1,0:T(4,128)S(1)} %copy-done, s32[4,4]{1,0:T(4,128)S(1)} %copy-done.1, s32[4]{0:T(128)S(1)} %copy-done.2, s32[2]{0:T(128)S(1)} %copy-done.3, bf16[32,3,2,8,1024]{4,3,2,1,0:T(8,128)(2,1)} %copy-done.6), custom_call_target="tpu_custom_call" | custom-call | flops 17999998976 | bytes 6291456 | tf_op jit(solution)/shard_map/unpack_early/pallas_call | solution.py:519
  346.6 35.8 %all-to-all-done.4.late_ref = bf16[32,3,2,8,1024]{4,3,2,1,0:T(8,128)(2,1)S(1)} async-done(((bf16[32,3,2,8,1024]{4,3,2,1,0:T(8,128)(2,1)}), bf16[32,3,2,8,1024]{4,3,2,1,0:T(8,128)(2,1)S(1)}, u32[]{:S(2)}, u32[]{:S(2)}) %all-to-all-start.4) | async-done | bytes 3145760 | tf_op jit(solution)/shard_map/all_to_all | solution.py:562
  382.4 6.9 %unpack.1 = bf16[3,1,4,2,1024,128]{5,4,3,2,1,0:T(8,128)(2,1)} custom-call(s32[4,4]{1,0:T(4,128)} %start_ref.3, s32[4,4]{1,0:T(4,128)} %frames_ref.3, s32[4]{0:T(128)} %count_ref.9, s32[2]{0:T(128)} %pad_add_fusion.place_ref, bf16[6,2,1024,128]{3,2,1,0:T(8,128)(2,1)} %unpack_early.1.part_ref, bf16[32,3,2,8,1024]{4,3,2,1,0:T(8,128)(2,1)S(1)} %all-to-all-done.4.late_ref), custom_call_target="tpu_custom_call" | custom-call | tf_op jit(solution)/shard_map/unpack/pallas_call | solution.py:540
  (16 shorter events, 0.0 us)
Async XLA Ops:
  8.0 40.0 %collective-permute-start = (bf16[2,3,1024,128]{3,2,1,0:T(8,128)(2,1)}, bf16[2,3,1024,128]{3,2,1,0:T(8,128)(2,1)S(1)}, u32[]{:S(2)}, u32[]{:S(2)}) collective-permute-start(bf16[2,3,1024,128]{3,2,1,0:T(8,128)(2,1)} %get-tuple-element.36), channel_id=1, source_target_pairs={{0,1},{1,2},{2,3},{3,0},{4,5},{5,6},{6,7},{7,4},{8,9},{9,10},{10,1... | collective-permute-start | bytes 4718600 | tf_op jit(solution)/shard_map/ppermute | solution.py:567
  8.9 74.1 %collective-permute-start.1 = (bf16[2,3,1024,128]{3,2,1,0:T(8,128)(2,1)}, bf16[2,3,1024,128]{3,2,1,0:T(8,128)(2,1)}, u32[]{:S(2)}, u32[]{:S(2)}) collective-permute-start(bf16[2,3,1024,128]{3,2,1,0:T(8,128)(2,1)} %get-tuple-element.37), channel_id=1, source_target_pairs={{0,2},{1,3},{2,0},{3,1},{4,6},{5,7},{6,4},{7,5},{8,10},{9,11},{10,... | collective-permute-start | bytes 4718600 | tf_op jit(solution)/shard_map/ppermute | solution.py:567
  14.8 68.2 %collective-permute-start.2 = (bf16[2,3,1024,128]{3,2,1,0:T(8,128)(2,1)}, bf16[2,3,1024,128]{3,2,1,0:T(8,128)(2,1)}, u32[]{:S(2)}, u32[]{:S(2)}) collective-permute-start(bf16[2,3,1024,128]{3,2,1,0:T(8,128)(2,1)} %get-tuple-element.38), channel_id=1, source_target_pairs={{0,3},{1,0},{2,1},{3,2},{4,7},{5,4},{6,5},{7,6},{8,11},{9,8},{10,9... | collective-permute-start | bytes 4718600 | tf_op jit(solution)/shard_map/ppermute | solution.py:567
  14.8 8.6 %copy-start.7 = (s32[5]{0:T(128)S(1)}, s32[5]{0:T(128)}, u32[]{:S(2)}) copy-start(s32[5]{0:T(128)} %get-tuple-element.33.plan_ref) | copy-start | bytes 64
  14.8 72.6 %all-to-all-start.1 = ((bf16[32,3,3,8,1024]{4,3,2,1,0:T(8,128)(2,1)}), bf16[32,3,3,8,1024]{4,3,2,1,0:T(8,128)(2,1)}, u32[]{:S(2)}, u32[]{:S(2)}) async-start(bf16[32,3,3,8,1024]{4,3,2,1,0:T(8,128)(2,1)} %get-tuple-element.30), calls=%async_computation.1 | async-start | bytes 9437184 | tf_op jit(solution)/shard_map/all_to_all | solution.py:562
  48.0 35.0 %copy-start.8 = (bf16[2,3,1024,128]{3,2,1,0:T(8,128)(2,1)}, bf16[2,3,1024,128]{3,2,1,0:T(8,128)(2,1)S(1)}, u32[]{:S(2)}) copy-start(bf16[2,3,1024,128]{3,2,1,0:T(8,128)(2,1)S(1)} %collective-permute-done.a1) | copy-start | bytes 4718596
  83.0 4.5 %copy-start.4 = (bf16[32,1,3,8,1024]{4,3,2,1,0:T(8,128)(2,1)S(1)}, bf16[32,1,3,8,1024]{4,3,2,1,0:T(8,128)(2,1)}, u32[]{:S(2)}) copy-start(bf16[32,1,3,8,1024]{4,3,2,1,0:T(8,128)(2,1)} %get-tuple-element.34) | copy-start | bytes 4718596
  87.5 1.1 copy-start.5
  88.6 157.4 %all-to-all-start.2 = ((bf16[32,2,3,8,1024]{4,3,2,1,0:T(8,128)(2,1)}), bf16[32,2,3,8,1024]{4,3,2,1,0:T(8,128)(2,1)S(1)}, u32[]{:S(2)}, u32[]{:S(2)}) async-start(bf16[32,2,3,8,1024]{4,3,2,1,0:T(8,128)(2,1)} %choose.1), calls=%async_computation.2 | async-start | bytes 6291456 | tf_op jit(solution)/shard_map/all_to_all | solution.py:562
  241.7 38.2 %collective-permute-start.3 = (bf16[32,3,8,1024]{3,2,1,0:T(8,128)(2,1)}, bf16[32,3,8,1024]{3,2,1,0:T(8,128)(2,1)}, u32[]{:S(2)}, u32[]{:S(2)}) collective-permute-start(bf16[32,3,8,1024]{3,2,1,0:T(8,128)(2,1)} %get-tuple-element.42), channel_id=1, source_target_pairs={{0,1},{1,2},{2,3},{3,0},{4,5},{5,6},{6,7},{7,4},{8,9},{9,10},{10,1... | collective-permute-start | bytes 4718600 | tf_op jit(solution)/shard_map/ppermute | solution.py:567
  241.8 72.8 %collective-permute-start.4 = (bf16[32,3,8,1024]{3,2,1,0:T(8,128)(2,1)}, bf16[32,3,8,1024]{3,2,1,0:T(8,128)(2,1)}, u32[]{:S(2)}, u32[]{:S(2)}) collective-permute-start(bf16[32,3,8,1024]{3,2,1,0:T(8,128)(2,1)} %get-tuple-element.43), channel_id=1, source_target_pairs={{0,2},{1,3},{2,0},{3,1},{4,6},{5,7},{6,4},{7,5},{8,10},{9,11},{10,... | collective-permute-start | bytes 4718600 | tf_op jit(solution)/shard_map/ppermute | solution.py:567
  246.0 68.6 %collective-permute-start.5 = (bf16[32,3,8,1024]{3,2,1,0:T(8,128)(2,1)}, bf16[32,3,8,1024]{3,2,1,0:T(8,128)(2,1)}, u32[]{:S(2)}, u32[]{:S(2)}) collective-permute-start(bf16[32,3,8,1024]{3,2,1,0:T(8,128)(2,1)} %get-tuple-element.44), channel_id=1, source_target_pairs={{0,3},{1,0},{2,1},{3,2},{4,7},{5,4},{6,5},{7,6},{8,11},{9,8},{10,9... | collective-permute-start | bytes 4718600 | tf_op jit(solution)/shard_map/ppermute | solution.py:567
  258.4 73.3 %all-to-all-start.3 = ((bf16[32,3,2,8,1024]{4,3,2,1,0:T(8,128)(2,1)}), bf16[32,3,2,8,1024]{4,3,2,1,0:T(8,128)(2,1)S(1)}, u32[]{:S(2)}, u32[]{:S(2)}) async-start(bf16[32,3,2,8,1024]{4,3,2,1,0:T(8,128)(2,1)} %filter_early.1), calls=%async_computation.3 | async-start | bytes 6291456 | tf_op jit(solution)/shard_map/all_to_all | solution.py:562
  331.7 9.0 %copy-start = (s32[4,4]{1,0:T(4,128)S(1)}, s32[4,4]{1,0:T(4,128)}, u32[]{:S(2)}) copy-start(s32[4,4]{1,0:T(4,128)} %start_ref.3) | copy-start | bytes 196
  331.7 8.9 %copy-start.1 = (s32[4,4]{1,0:T(4,128)S(1)}, s32[4,4]{1,0:T(4,128)}, u32[]{:S(2)}) copy-start(s32[4,4]{1,0:T(4,128)} %frames_ref.3) | copy-start | bytes 196
  331.7 8.9 %copy-start.2 = (s32[4]{0:T(128)S(1)}, s32[4]{0:T(128)}, u32[]{:S(2)}) copy-start(s32[4]{0:T(128)} %count_ref.9) | copy-start | bytes 52
  331.8 8.9 %copy-start.3 = (s32[2]{0:T(128)S(1)}, s32[2]{0:T(128)}, u32[]{:S(2)}) copy-start(s32[2]{0:T(128)} %pad_add_fusion.place_ref) | copy-start | bytes 28
  331.8 1.7 copy-start.6
  333.4 49.0 %all-to-all-start.4 = ((bf16[32,3,2,8,1024]{4,3,2,1,0:T(8,128)(2,1)}), bf16[32,3,2,8,1024]{4,3,2,1,0:T(8,128)(2,1)S(1)}, u32[]{:S(2)}, u32[]{:S(2)}) async-start(bf16[32,3,2,8,1024]{4,3,2,1,0:T(8,128)(2,1)} %filter_late.1), calls=%async_computation.4 | async-start | bytes 6291456 | tf_op jit(solution)/shard_map/all_to_all | solution.py:562
where the time goes:
time: 390 us; the launch traced here: 389 us
  Pallas kernels  199 us (51%)
  waiting for transfers between devices  143 us (37%)
  starting transfers between devices  42.7 us (11%)
    pallas_call x1, Pallas kernels, split(): pl.pallas_call(split_kernel, out_shape=[jax.ShapeDtypeStruct((TM, HOPS_DE...  145 us
    ppermute x6, waiting for transfers between devices, along_chan(): lax.ppermute(in_hbm(arrays[d]), 'chan', [(s, (s + d) % OWNERS) for s in r...  107 us
    all_to_all x4, waiting for transfers between devices, over_tm(): return lax.all_to_all(array, 'tm', split_axis=0, concat_axis=0, tiled=True)  35.8 us
    all_to_all x4, starting transfers between devices, over_tm(): return lax.all_to_all(array, 'tm', split_axis=0, concat_axis=0, tiled=True)  31.5 us
    pallas_call x1, Pallas kernels, filter_late(): pl.pallas_call(late_kernel, out_shape=RESULT, grid_spec=pltpu.PrefetchSca...  17.1 us
    pallas_call x1, Pallas kernels, filter_early(): pl.pallas_call(early_kernel, out_shape=RESULT, grid=(MAXREQ // 2,), in_sp...  12.4 us
    ppermute x6, starting transfers between devices, along_chan(): lax.ppermute(in_hbm(arrays[d]), 'chan', [(s, (s + d) % OWNERS) for s in r...  11.2 us
  transfers between devices with their start and end apart: 10, of which 5 were waited for; matrix products, arithmetic and copies ran while one was open for 0% of the time, Pallas kernels for 47%

commit v1 on v0

--- a/solution.py
+++ b/solution.py
@@ -191,20 +191,23 @@
 
 
 def split_kernel(plan_ref, late_ref, last_ref, *refs):
-    out_refs, sem = refs[:-1], refs[-1]
-    for d, out_ref in enumerate(out_refs, 1):
+    *out_refs, held_ref, in_sem, out_sem = refs
+    for d in range(1, OWNERS):
         group = plan_ref[d]
 
         @pl.when(group < OWNERS - 1)
         def _():
-            pltpu.make_async_copy(late_ref.at[:, group], out_ref, sem.at[d]).start()
+            pltpu.make_async_copy(late_ref.at[:, group], held_ref.at[d - 1], in_sem.at[d - 1]).start()
 
         @pl.when(group >= OWNERS - 1)
         def _():
-            pltpu.make_async_copy(last_ref.at[:, 0], out_ref, sem.at[d]).start()
-
-    for d, out_ref in enumerate(out_refs, 1):
-        pltpu.make_async_copy(last_ref.at[:, 0], out_ref, sem.at[d]).wait()
+            pltpu.make_async_copy(last_ref.at[:, 0], held_ref.at[d - 1], in_sem.at[d - 1]).start()
+
+    for at, out_ref in enumerate(out_refs):
+        pltpu.make_async_copy(last_ref.at[:, 0], held_ref.at[at], in_sem.at[at]).wait()
+        pltpu.make_async_copy(held_ref.at[at], out_ref, out_sem.at[at]).start()
+    for at, out_ref in enumerate(out_refs):
+        pltpu.make_async_copy(held_ref.at[at], out_ref, out_sem.at[at]).wait()
 
 
 def split(plan, late, last):
@@ -217,7 +220,11 @@
             grid=(1,),
             in_specs=[anywhere] * 2,
             out_specs=[anywhere] * (OWNERS - 1),
-            scratch_shapes=[pltpu.SemaphoreType.DMA((OWNERS,))],
+            scratch_shapes=[
+                pltpu.VMEM((OWNERS - 1, TM, HOPS_DEV, ROWS, NFINE), jnp.bfloat16),
+                pltpu.SemaphoreType.DMA((OWNERS - 1,)),
+                pltpu.SemaphoreType.DMA((OWNERS - 1,)),
+            ],
         ),
         name="split",
     )(plan, in_hbm(late), in_hbm(last))

time: 390 us -> 252 us (0.65)
  Pallas kernels: 199 us -> 60.5 us
  starting transfers between devices: 42.7 us -> 32.7 us
  waiting for transfers between devices: 143 us -> 153 us
    pallas_call x1, Pallas kernels: 145 us -> 4.26 us  [split(): pl.pallas_call(split_kernel, out_shape=[jax.ShapeDtypeStruct((TM, HOPS_DE...]
    all_to_all x4, waiting for transfers between devices: 35.8 us -> 77 us  [over_tm(): return lax.all_to_all(array, 'tm', split_axis=0, concat_axis=0, tiled=True)]
    ppermute x6, waiting for transfers between devices: 107 us -> 76.4 us  [along_chan(): lax.ppermute(in_hbm(arrays[d]), 'chan', [(s, (s + d) % OWNERS) for s in r...]
    all_to_all x4, starting transfers between devices: 31.5 us -> 26 us  [over_tm(): return lax.all_to_all(array, 'tm', split_axis=0, concat_axis=0, tiled=True)]
    ppermute x6, starting transfers between devices: 11.2 us -> 6.75 us  [along_chan(): lax.ppermute(in_hbm(arrays[d]), 'chan', [(s, (s + d) % OWNERS) for s in r...]
  transfers between devices with their start and end apart: 10 -> 10, of which waited for: 5 -> 7; matrix products, arithmetic and copies ran while one was open for 0% -> 0% of each run, Pallas kernels for 47% -> 17%
where the time goes in v1:
time: 252 us
  waiting for transfers between devices  153 us (61%)
  Pallas kernels  60.5 us (24%)
  starting transfers between devices  32.7 us (13%)
  local copies, waits for them, and re-layouts  3.95 us (2%)
    all_to_all x4, waiting for transfers between devices, over_tm(): return lax.all_to_all(array, 'tm', split_axis=0, concat_axis=0, tiled=True)  77 us
    ppermute x6, waiting for transfers between devices, along_chan(): lax.ppermute(in_hbm(arrays[d]), 'chan', [(s, (s + d) % OWNERS) for s in r...  76.4 us
    all_to_all x4, starting transfers between devices, over_tm(): return lax.all_to_all(array, 'tm', split_axis=0, concat_axis=0, tiled=True)  26 us
    pallas_call x1, Pallas kernels, filter_late(): pl.pallas_call(late_kernel, out_shape=RESULT, grid_spec=pltpu.PrefetchSca...  16.1 us
    pallas_call x1, Pallas kernels, filter_early(): pl.pallas_call(early_kernel, out_shape=RESULT, grid=(MAXREQ // 2,), in_sp...  12.4 us
    pallas_call x1, Pallas kernels, pack(): pl.pallas_call(pack_kernel, out_shape=[jax.ShapeDtypeStruct((OWNERS + 1,)...  10.5 us
    pallas_call x1, Pallas kernels, unpack(): pl.pallas_call(unpack_kernel, out_shape=jax.ShapeDtypeStruct((HOPS_DEV, 1...  6.85 us
    ppermute x6, starting transfers between devices, along_chan(): lax.ppermute(in_hbm(arrays[d]), 'chan', [(s, (s + d) % OWNERS) for s in r...  6.75 us
  transfers between devices with their start and end apart: 10, of which 7 were waited for; matrix products, arithmetic and copies ran while one was open for 0% of the time, Pallas kernels for 17%

profile of v1, /device:TPU:0, one launch (start us, length us, event | category | flops | bytes accessed | tf_op | source)
XLA Modules:
  0.0 252.1 jit_solution(16600148542758120651)
XLA Ops:
  0.0 0.6 pad_add_fusion.place_ref
  0.6 10.5 %pack.1 = (s32[5]{0:T(128)}, bf16[32,3,3,8,1024]{4,3,2,1,0:T(8,128)(2,1)}, bf16[32,1,3,8,1024]{4,3,2,1,0:T(8,128)(2,1)}, bf16[2,3,1024,128]{3,2,1,0:T(8,128)(2,1...) custom-call(s32[4,4]{1,0:T(4,128)} %block_ref.5, ...), custom_call_target="tpu_custom_call" | custom-call | tf_op jit(solution)/shard_map/pack/pallas_call | solution.py:158
  11.1 0.1 collective-permute-start
  11.2 2.3 collective-permute-start.1
  13.5 0.9 collective-permute-start.2
  14.4 8.7 %all-to-all-start.1 = ((bf16[32,3,3,8,1024]{4,3,2,1,0:T(8,128)(2,1)}), bf16[32,3,3,8,1024]{4,3,2,1,0:T(8,128)(2,1)}, u32[]{:S(2)}, u32[]{:S(2)}) async-start(bf16[32,3,3,8,1024]{4,3,2,1,0:T(8,128)(2,1)} %get-tuple-element.30), calls=%async_computation.1 | async-start | bytes 9437184 | tf_op jit(solution)/shard_map/all_to_all | solution.py:569
  23.1 0.7 slice.3
  24.5 57.2 %collective-permute-done.a1 = bf16[2,3,1024,128]{3,2,1,0:T(8,128)(2,1)S(1)} collective-permute-done((bf16[2,3,1024,128]{3,2,1,0:T(8,128)(2,1)}, bf16[2,3,1024,128]{3,2,1,0:T(8,128)(2,1)S(1)}, u32[]{:S(2)}, u32[]{:S(2)}) %collective-permute-start) | collective-permute-done | bytes 1572896 | tf_op jit(solution)/shard_map/ppermute | solution.py:574
  81.7 0.0 collective-permute-done.1.a2
  81.7 0.7 collective-permute-done.2.a3
  82.4 0.5 copy-done.8
  82.9 4.4 %choose.1 = bf16[32,2,3,8,1024]{4,3,2,1,0:T(8,128)(2,1)} custom-call(s32[4,4]{1,0:T(4,128)} %block_ref.5, s32[4]{0:T(128)} %count_ref.9, s32[2]{0:T(128)} %pad_add_fusion.place_ref, bf16[2,3,1024,128]{3,2,1,0:T(8,128)(2,1)} %get-tuple-element.35.a0, bf16[2,3,1024,128]{3,2,1,0:T(8,128)(2,1)} %copy-done.8, ...), custom_call_target="tpu_custom_call" | custom-call | flops 149999992832 | bytes 4194304 | tf_op jit(solution)/shard_map/choose/pallas_call | solution.py:275
  87.4 0.0 copy-start.5
  87.4 1.1 copy-done.5
  88.5 9.2 %all-to-all-start.2 = ((bf16[32,2,3,8,1024]{4,3,2,1,0:T(8,128)(2,1)}), bf16[32,2,3,8,1024]{4,3,2,1,0:T(8,128)(2,1)S(1)}, u32[]{:S(2)}, u32[]{:S(2)}) async-start(bf16[32,2,3,8,1024]{4,3,2,1,0:T(8,128)(2,1)} %choose.1), calls=%async_computation.2 | async-start | bytes 6291456 | tf_op jit(solution)/shard_map/all_to_all | solution.py:569
  97.7 4.3 %split.1 = (bf16[32,3,8,1024]{3,2,1,0:T(8,128)(2,1)}, bf16[32,3,8,1024]{3,2,1,0:T(8,128)(2,1)}, bf16[32,3,8,1024]{3,2,1,0:T(8,128)(2,1)}) custom-call(s32[5]{0:T(128)} %get-tuple-element.33.plan_ref, bf16[32,3,3,8,1024]{4,3,2,1,0:T(8,128)(2,1)} %all-to-all-done.1.late_ref.a0, bf16[32,1,3,8,1024]{4,3,2,1,0:T(8,128)(2,1)} %copy-done.5), custom_call_target="tpu_custom_call" | custom-call | tf_op jit(solution)/shard_map/split/pallas_call | solution.py:215
  102.0 0.1 collective-permute-start.3
  102.0 3.4 %collective-permute-start.4 = (bf16[32,3,8,1024]{3,2,1,0:T(8,128)(2,1)}, bf16[32,3,8,1024]{3,2,1,0:T(8,128)(2,1)}, u32[]{:S(2)}, u32[]{:S(2)}) collective-permute-start(bf16[32,3,8,1024]{3,2,1,0:T(8,128)(2,1)} %get-tuple-element.43), channel_id=1, source_target_pairs={{0,2},{1,3},{2,0},{3,1},{4,6},{5,7},{6,4},{7,5},{8,10},{9,11},{10,... | collective-permute-start | bytes 4718600 | tf_op jit(solution)/shard_map/ppermute | solution.py:574
  105.4 0.0 collective-permute-start.5
  105.4 34.0 %all-to-all-done.2.x_ref = bf16[32,2,3,8,1024]{4,3,2,1,0:T(8,128)(2,1)S(1)} async-done(((bf16[32,2,3,8,1024]{4,3,2,1,0:T(8,128)(2,1)}), bf16[32,2,3,8,1024]{4,3,2,1,0:T(8,128)(2,1)S(1)}, u32[]{:S(2)}, u32[]{:S(2)}) %all-to-all-start.2) | async-done | bytes 3145760 | tf_op jit(solution)/shard_map/all_to_all | solution.py:569
  139.5 12.4 %filter_early.1 = bf16[32,3,2,8,1024]{4,3,2,1,0:T(8,128)(2,1)} custom-call(bf16[32,2,3,8,1024]{4,3,2,1,0:T(8,128)(2,1)S(1)} %all-to-all-done.2.x_ref, f32[16,1024]{1,0:T(8,128)} %proto_ref.1, bf16[8,128,256]{2,1,0:T(8,128)(2,1)} %constant.16.clone.refs_1_.high_ref, bf16[8,128,256]{2,1,0:T(8,128)(2,1)} %constant.17.clone.refs_2_.low_ref), custom_call_target="tpu_custom_call" | custom-call | flops 17999998976 | bytes 6291456 | tf_op jit(solution)/shard_map/filter_early/pallas_call | solution.py:426
  151.9 4.1 %all-to-all-start.3 = ((bf16[32,3,2,8,1024]{4,3,2,1,0:T(8,128)(2,1)}), bf16[32,3,2,8,1024]{4,3,2,1,0:T(8,128)(2,1)S(1)}, u32[]{:S(2)}, u32[]{:S(2)}) async-start(bf16[32,3,2,8,1024]{4,3,2,1,0:T(8,128)(2,1)} %filter_early.1), calls=%async_computation.3 | async-start | bytes 6291456 | tf_op jit(solution)/shard_map/all_to_all | solution.py:569
  155.9 18.0 %collective-permute-done.4.a2 = bf16[32,3,8,1024]{3,2,1,0:T(8,128)(2,1)} collective-permute-done((bf16[32,3,8,1024]{3,2,1,0:T(8,128)(2,1)}, bf16[32,3,8,1024]{3,2,1,0:T(8,128)(2,1)}, u32[]{:S(2)}, u32[]{:S(2)}) %collective-permute-start.4) | collective-permute-done | bytes 1572896 | tf_op jit(solution)/shard_map/ppermute | solution.py:574
  174.0 0.5 collective-permute-done.5.a3
  174.5 16.1 %filter_late.1 = bf16[32,3,2,8,1024]{4,3,2,1,0:T(8,128)(2,1)} custom-call(s32[4,4]{1,0:T(4,128)} %block_ref.5, s32[4]{0:T(128)} %count_ref.9, s32[2]{0:T(128)} %pad_add_fusion.place_ref, bf16[32,3,3,8,1024]{4,3,2,1,0:T(8,128)(2,1)} %all-to-all-done.1.late_ref.a0, bf16[32,3,8,1024]{3,2,1,0:T(8,128)(2,1)} %collective-permute-done.3.a1, ...), custom_call_target="tpu_custom_call" | custom-call | flops 17999998976 | bytes 6291456 | tf_op jit(solution)/shard_map/filter_late/pallas_call | solution.py:442
  190.6 0.0 copy-start
  190.6 7.1 %all-to-all-done.3.early_ref = bf16[32,3,2,8,1024]{4,3,2,1,0:T(8,128)(2,1)S(1)} async-done(((bf16[32,3,2,8,1024]{4,3,2,1,0:T(8,128)(2,1)}), bf16[32,3,2,8,1024]{4,3,2,1,0:T(8,128)(2,1)S(1)}, u32[]{:S(2)}, u32[]{:S(2)}) %all-to-all-start.3) | async-done | bytes 3145760 | tf_op jit(solution)/shard_map/all_to_all | solution.py:569
  197.7 1.7 copy-done.6
  199.4 4.1 %all-to-all-start.4 = ((bf16[32,3,2,8,1024]{4,3,2,1,0:T(8,128)(2,1)}), bf16[32,3,2,8,1024]{4,3,2,1,0:T(8,128)(2,1)S(1)}, u32[]{:S(2)}, u32[]{:S(2)}) async-start(bf16[32,3,2,8,1024]{4,3,2,1,0:T(8,128)(2,1)} %filter_late.1), calls=%async_computation.4 | async-start | bytes 6291456 | tf_op jit(solution)/shard_map/all_to_all | solution.py:569
  203.5 5.9 %unpack_early.1.part_ref = bf16[6,2,1024,128]{3,2,1,0:T(8,128)(2,1)} custom-call(s32[4,4]{1,0:T(4,128)S(1)} %copy-done, s32[4,4]{1,0:T(4,128)S(1)} %copy-done.1, s32[4]{0:T(128)S(1)} %copy-done.2, s32[2]{0:T(128)S(1)} %copy-done.3, bf16[32,3,2,8,1024]{4,3,2,1,0:T(8,128)(2,1)} %copy-done.6), custom_call_target="tpu_custom_call" | custom-call | flops 17999998976 | bytes 6291456 | tf_op jit(solution)/shard_map/unpack_early/pallas_call | solution.py:526
  209.4 35.8 %all-to-all-done.4.late_ref = bf16[32,3,2,8,1024]{4,3,2,1,0:T(8,128)(2,1)S(1)} async-done(((bf16[32,3,2,8,1024]{4,3,2,1,0:T(8,128)(2,1)}), bf16[32,3,2,8,1024]{4,3,2,1,0:T(8,128)(2,1)S(1)}, u32[]{:S(2)}, u32[]{:S(2)}) %all-to-all-start.4) | async-done | bytes 3145760 | tf_op jit(solution)/shard_map/all_to_all | solution.py:569
  245.2 6.9 %unpack.1 = bf16[3,1,4,2,1024,128]{5,4,3,2,1,0:T(8,128)(2,1)} custom-call(s32[4,4]{1,0:T(4,128)} %start_ref.3, s32[4,4]{1,0:T(4,128)} %frames_ref.3, s32[4]{0:T(128)} %count_ref.9, s32[2]{0:T(128)} %pad_add_fusion.place_ref, bf16[6,2,1024,128]{3,2,1,0:T(8,128)(2,1)} %unpack_early.1.part_ref, bf16[32,3,2,8,1024]{4,3,2,1,0:T(8,128)(2,1)S(1)} %all-to-all-done.4.late_ref), custom_call_target="tpu_custom_call" | custom-call | tf_op jit(solution)/shard_map/unpack/pallas_call | solution.py:547
  (16 shorter events, 0.0 us)
Async XLA Ops:
  11.1 70.6 %collective-permute-start = (bf16[2,3,1024,128]{3,2,1,0:T(8,128)(2,1)}, bf16[2,3,1024,128]{3,2,1,0:T(8,128)(2,1)S(1)}, u32[]{:S(2)}, u32[]{:S(2)}) collective-permute-start(bf16[2,3,1024,128]{3,2,1,0:T(8,128)(2,1)} %get-tuple-element.36), channel_id=1, source_target_pairs={{0,1},{1,2},{2,3},{3,0},{4,5},{5,6},{6,7},{7,4},{8,9},{9,10},{10,1... | collective-permute-start | bytes 4718600 | tf_op jit(solution)/shard_map/ppermute | solution.py:574
  11.2 70.5 %collective-permute-start.1 = (bf16[2,3,1024,128]{3,2,1,0:T(8,128)(2,1)}, bf16[2,3,1024,128]{3,2,1,0:T(8,128)(2,1)}, u32[]{:S(2)}, u32[]{:S(2)}) collective-permute-start(bf16[2,3,1024,128]{3,2,1,0:T(8,128)(2,1)} %get-tuple-element.37), channel_id=1, source_target_pairs={{0,2},{1,3},{2,0},{3,1},{4,6},{5,7},{6,4},{7,5},{8,10},{9,11},{10,... | collective-permute-start | bytes 4718600 | tf_op jit(solution)/shard_map/ppermute | solution.py:574
  13.5 68.9 %collective-permute-start.2 = (bf16[2,3,1024,128]{3,2,1,0:T(8,128)(2,1)}, bf16[2,3,1024,128]{3,2,1,0:T(8,128)(2,1)}, u32[]{:S(2)}, u32[]{:S(2)}) collective-permute-start(bf16[2,3,1024,128]{3,2,1,0:T(8,128)(2,1)} %get-tuple-element.38), channel_id=1, source_target_pairs={{0,3},{1,0},{2,1},{3,2},{4,7},{5,4},{6,5},{7,6},{8,11},{9,8},{10,9... | collective-permute-start | bytes 4718600 | tf_op jit(solution)/shard_map/ppermute | solution.py:574
  14.4 8.7 %copy-start.7 = (s32[5]{0:T(128)S(1)}, s32[5]{0:T(128)}, u32[]{:S(2)}) copy-start(s32[5]{0:T(128)} %get-tuple-element.33.plan_ref) | copy-start | bytes 64
  14.4 72.9 %all-to-all-start.1 = ((bf16[32,3,3,8,1024]{4,3,2,1,0:T(8,128)(2,1)}), bf16[32,3,3,8,1024]{4,3,2,1,0:T(8,128)(2,1)}, u32[]{:S(2)}, u32[]{:S(2)}) async-start(bf16[32,3,3,8,1024]{4,3,2,1,0:T(8,128)(2,1)} %get-tuple-element.30), calls=%async_computation.1 | async-start | bytes 9437184 | tf_op jit(solution)/shard_map/all_to_all | solution.py:569
  81.7 1.2 copy-start.8
  82.9 4.4 %copy-start.4 = (bf16[32,1,3,8,1024]{4,3,2,1,0:T(8,128)(2,1)S(1)}, bf16[32,1,3,8,1024]{4,3,2,1,0:T(8,128)(2,1)}, u32[]{:S(2)}) copy-start(bf16[32,1,3,8,1024]{4,3,2,1,0:T(8,128)(2,1)} %get-tuple-element.34) | copy-start | bytes 4718596
  87.4 1.1 copy-start.5
  88.5 50.9 %all-to-all-start.2 = ((bf16[32,2,3,8,1024]{4,3,2,1,0:T(8,128)(2,1)}), bf16[32,2,3,8,1024]{4,3,2,1,0:T(8,128)(2,1)S(1)}, u32[]{:S(2)}, u32[]{:S(2)}) async-start(bf16[32,2,3,8,1024]{4,3,2,1,0:T(8,128)(2,1)} %choose.1), calls=%async_computation.2 | async-start | bytes 6291456 | tf_op jit(solution)/shard_map/all_to_all | solution.py:569
  102.0 54.0 %collective-permute-start.3 = (bf16[32,3,8,1024]{3,2,1,0:T(8,128)(2,1)}, bf16[32,3,8,1024]{3,2,1,0:T(8,128)(2,1)}, u32[]{:S(2)}, u32[]{:S(2)}) collective-permute-start(bf16[32,3,8,1024]{3,2,1,0:T(8,128)(2,1)} %get-tuple-element.42), channel_id=1, source_target_pairs={{0,1},{1,2},{2,3},{3,0},{4,5},{5,6},{6,7},{7,4},{8,9},{9,10},{10,1... | collective-permute-start | bytes 4718600 | tf_op jit(solution)/shard_map/ppermute | solution.py:574
  102.0 71.9 %collective-permute-start.4 = (bf16[32,3,8,1024]{3,2,1,0:T(8,128)(2,1)}, bf16[32,3,8,1024]{3,2,1,0:T(8,128)(2,1)}, u32[]{:S(2)}, u32[]{:S(2)}) collective-permute-start(bf16[32,3,8,1024]{3,2,1,0:T(8,128)(2,1)} %get-tuple-element.43), channel_id=1, source_target_pairs={{0,2},{1,3},{2,0},{3,1},{4,6},{5,7},{6,4},{7,5},{8,10},{9,11},{10,... | collective-permute-start | bytes 4718600 | tf_op jit(solution)/shard_map/ppermute | solution.py:574
  105.4 69.0 %collective-permute-start.5 = (bf16[32,3,8,1024]{3,2,1,0:T(8,128)(2,1)}, bf16[32,3,8,1024]{3,2,1,0:T(8,128)(2,1)}, u32[]{:S(2)}, u32[]{:S(2)}) collective-permute-start(bf16[32,3,8,1024]{3,2,1,0:T(8,128)(2,1)} %get-tuple-element.44), channel_id=1, source_target_pairs={{0,3},{1,0},{2,1},{3,2},{4,7},{5,4},{6,5},{7,6},{8,11},{9,8},{10,9... | collective-permute-start | bytes 4718600 | tf_op jit(solution)/shard_map/ppermute | solution.py:574
  151.9 45.8 %all-to-all-start.3 = ((bf16[32,3,2,8,1024]{4,3,2,1,0:T(8,128)(2,1)}), bf16[32,3,2,8,1024]{4,3,2,1,0:T(8,128)(2,1)S(1)}, u32[]{:S(2)}, u32[]{:S(2)}) async-start(bf16[32,3,2,8,1024]{4,3,2,1,0:T(8,128)(2,1)} %filter_early.1), calls=%async_computation.3 | async-start | bytes 6291456 | tf_op jit(solution)/shard_map/all_to_all | solution.py:569
  190.6 12.9 %copy-start = (s32[4,4]{1,0:T(4,128)S(1)}, s32[4,4]{1,0:T(4,128)}, u32[]{:S(2)}) copy-start(s32[4,4]{1,0:T(4,128)} %start_ref.3) | copy-start | bytes 196
  190.6 12.9 %copy-start.1 = (s32[4,4]{1,0:T(4,128)S(1)}, s32[4,4]{1,0:T(4,128)}, u32[]{:S(2)}) copy-start(s32[4,4]{1,0:T(4,128)} %frames_ref.3) | copy-start | bytes 196
  190.6 12.9 %copy-start.2 = (s32[4]{0:T(128)S(1)}, s32[4]{0:T(128)}, u32[]{:S(2)}) copy-start(s32[4]{0:T(128)} %count_ref.9) | copy-start | bytes 52
  190.6 12.9 %copy-start.3 = (s32[2]{0:T(128)S(1)}, s32[2]{0:T(128)}, u32[]{:S(2)}) copy-start(s32[2]{0:T(128)} %pad_add_fusion.place_ref) | copy-start | bytes 28
  197.7 1.7 copy-start.6
  199.4 45.8 %all-to-all-start.4 = ((bf16[32,3,2,8,1024]{4,3,2,1,0:T(8,128)(2,1)}), bf16[32,3,2,8,1024]{4,3,2,1,0:T(8,128)(2,1)S(1)}, u32[]{:S(2)}, u32[]{:S(2)}) async-start(bf16[32,3,2,8,1024]{4,3,2,1,0:T(8,128)(2,1)} %filter_late.1), calls=%async_computation.4 | async-start | bytes 6291456 | tf_op jit(solution)/shard_map/all_to_all | solution.py:569
